TPU v7x, 256 devices: a whole 4x4x8 slice. The times are simulated.
256 devices in a mesh: gx: 16 (over y, z_lo, core), gy: 4 (over x), gz: 4 (over z_hi).
Axes of the slice: x: 4, y: 4, z: 8 (z_hi: 4, z_lo: 2; z = z_hi * 2 + z_lo), core: 2. Of those that a mesh axis runs over, the one named last changes fastest.
Arguments:
- features: bfloat16 [32, 64, 16, 1024], P(None, 'gx', 'gy', 'gz'), may hold values from -6 to 6
- conv_one: bfloat16 [32, 864], replicated, may hold values from -0.3125 to 0.3125
- conv_two: bfloat16 [32, 864], replicated, may hold values from -0.3125 to 0.3125
- conv_three: bfloat16 [64, 864], replicated, may hold values from -0.3125 to 0.3125
- conv_four: bfloat16 [64, 1728], replicated, may hold values from -0.21875 to 0.21875
- depth_one: bfloat16 [64, 27], replicated, may hold values from -1.25 to 1.25
- point_one: bfloat16 [128, 64], replicated, may hold values from -1 to 1
- depth_two: bfloat16 [128, 27], replicated, may hold values from -1.25 to 1.25
- point_two: bfloat16 [128, 128], replicated, may hold values from -0.75 to 0.75
- conv_five: bfloat16 [64, 5184], replicated, may hold values from -0.125 to 0.125
- conv_six: bfloat16 [32, 2592], replicated, may hold values from -0.125 to 0.125
Outputs:
- decoded: bfloat16 [32, 64, 16, 1024], P(None, 'gx', 'gy', 'gz')
All inputs are finite; a program needn't handle non-finite values.
Results may differ from a plain program's by a relative error of at most 0.015.
Values may be sent and summed in bfloat16 or wider, within the bound.
No kernel may reach another device: no remote copies, remote signals or barrier semaphores. Data moves between devices by JAX's collectives and lax.ppermute only.
A program may use at most 64 MiB of HBM per device.

v0:
```python
import jax
import jax.numpy as jnp
from jax import lax
from jax.sharding import PartitionSpec as P


def padded_2(cells, sides, width):
    for axis, dim in sides:
        count = lax.axis_size(axis)
        ends = count - 1
        head = lax.slice_in_dim(cells, 0, width, axis=dim)
        tail = lax.slice_in_dim(cells, cells.shape[dim] - width, cells.shape[dim], axis=dim)
        cells = jnp.concatenate(
            [
                lax.ppermute(tail, axis, [(i, (i + 1) % count) for i in range(ends)]),
                cells,
                lax.ppermute(head, axis, [((i + 1) % count, i) for i in range(ends)]),
            ],
            axis=dim,
        )
    return cells


def rectify(values):
    return jnp.maximum(values, 0.0)


def pad_faces(values):
    return padded_2(values, (("gx", 1), ("gy", 2), ("gz", 3)), 1)


def convolve(padded, weight):
    channels = padded.shape[0]
    width_out = weight.shape[0]
    size_x = padded.shape[1] - 2
    size_y = padded.shape[2] - 2
    size_z = padded.shape[3] - 2
    volume = size_x * size_y * size_z
    summed = jnp.zeros((width_out, volume), jnp.float32)
    for offset_x in range(3):
        for offset_y in range(3):
            for offset_z in range(3):
                tap_index = (offset_x * 3 + offset_y) * 3 + offset_z
                piece = padded[
                    :,
                    offset_x : offset_x + size_x,
                    offset_y : offset_y + size_y,
                    offset_z : offset_z + size_z,
                ].reshape(channels, volume)
                columns = weight[:, tap_index * channels : (tap_index + 1) * channels]
                summed = summed + jnp.dot(columns, piece, preferred_element_type=jnp.float32)
    return summed.reshape(width_out, size_x, size_y, size_z)


def depthwise(padded, tap_weights):
    size_x = padded.shape[1] - 2
    size_y = padded.shape[2] - 2
    size_z = padded.shape[3] - 2
    summed = jnp.zeros((padded.shape[0], size_x, size_y, size_z), jnp.float32)
    for offset_x in range(3):
        for offset_y in range(3):
            for offset_z in range(3):
                tap_index = (offset_x * 3 + offset_y) * 3 + offset_z
                factor = tap_weights[:, tap_index].astype(jnp.float32)[:, None, None, None]
                window = padded[
                    :,
                    offset_x : offset_x + size_x,
                    offset_y : offset_y + size_y,
                    offset_z : offset_z + size_z,
                ]
                summed = summed + window.astype(jnp.float32) * factor
    return summed.astype(jnp.bfloat16)


def shrink(values):
    channels, size_x, size_y, size_z = values.shape
    return values.reshape(channels, size_x // 2, 2, size_y // 2, 2, size_z // 2, 2).max(
        axis=(2, 4, 6)
    )


def enlarge(values):
    channels, size_x, size_y, size_z = values.shape
    grown = jnp.broadcast_to(
        values[:, :, None, :, None, :, None], (channels, size_x, 2, size_y, 2, size_z, 2)
    )
    return grown.reshape(channels, 2 * size_x, 2 * size_y, 2 * size_z)


def conv_pair(values, weight_a, weight_b):
    middle = rectify(convolve(pad_faces(values), weight_a)).astype(jnp.bfloat16)
    return rectify(convolve(pad_faces(middle), weight_b)).astype(jnp.bfloat16)


def channel_depthwise(values, tap_weights):
    channels, size_x, size_y, size_z = values.shape
    planes = lax.axis_size(("gx", "gy"))
    rows_x = lax.axis_size("gx")
    rows_y = lax.axis_size("gy")
    per_device = channels // planes
    volume = size_x * size_y * size_z
    outgoing = values.reshape(1, channels, volume)
    arrived = lax.all_to_all(outgoing, ("gx", "gy"), split_axis=1, concat_axis=0, tiled=True)
    arranged = arrived.reshape(rows_x, rows_y, per_device, size_x, size_y, size_z).transpose(
        2, 0, 3, 1, 4, 5
    )
    arranged = arranged.reshape(per_device, rows_x * size_x, rows_y * size_y, size_z)
    rimmed = padded_2(arranged, (("gz", 3),), 1)
    padded = jnp.pad(rimmed, ((0, 0), (1, 1), (1, 1), (0, 0)))
    own_taps = lax.dynamic_slice_in_dim(
        tap_weights, lax.axis_index(("gx", "gy")) * per_device, per_device, 0
    )
    spread = depthwise(padded, own_taps)
    outgoing_back = spread.reshape(per_device, rows_x, size_x, rows_y, size_y, size_z).transpose(
        1, 3, 0, 2, 4, 5
    )
    outgoing_back = outgoing_back.reshape(planes, per_device, volume)
    returned = lax.all_to_all(outgoing_back, ("gx", "gy"), split_axis=0, concat_axis=1, tiled=True)
    return returned.reshape(channels, size_x, size_y, size_z)


def quarter_layer(values, tap_weights, mixing):
    channels, size_x, size_y, size_z = values.shape
    spread = channel_depthwise(values, tap_weights)
    flattened = spread.reshape(channels, size_x * size_y * size_z)
    mixed_out = rectify(jnp.dot(mixing, flattened, preferred_element_type=jnp.float32))
    return mixed_out.astype(jnp.bfloat16).reshape(mixing.shape[0], size_x, size_y, size_z)


def decoder_input(coarse, fine_skip):
    return pad_faces(jnp.concatenate([enlarge(coarse), fine_skip], axis=0))


def local(
    features,
    conv_one,
    conv_two,
    conv_three,
    conv_four,
    depth_one,
    point_one,
    depth_two,
    point_two,
    conv_five,
    conv_six,
):
    skip = conv_pair(features, conv_one, conv_two)
    half_in = shrink(skip)
    half_skip = conv_pair(half_in, conv_three, conv_four)
    quarter = shrink(half_skip)
    mixed_one = quarter_layer(quarter, depth_one, point_one)
    mixed_two = quarter_layer(mixed_one, depth_two, point_two)
    half_out = rectify(convolve(decoder_input(mixed_two, half_skip), conv_five)).astype(
        jnp.bfloat16
    )
    return convolve(decoder_input(half_out, skip), conv_six).astype(jnp.bfloat16)


def solution(mesh):
    in_specs = (P(None, "gx", "gy", "gz"), P(), P(), P(), P(), P(), P(), P(), P(), P(), P())
    out_specs = P(None, "gx", "gy", "gz")
    return jax.shard_map(local, mesh=mesh, in_specs=in_specs, out_specs=out_specs, check_vma=False)
```

profile of v0, /device:TPU:72, one launch (start us, length us, event | category | flops | bytes accessed | tf_op | source)
XLA Modules:
  0.0 486.0 jit_solution(7746145017843126168)
XLA Ops:
  2.9 4.5 collective-permute-start.1
  11.1 3.4 collective-permute-start.2
  19.6 4.5 collective-permute-done.3
  27.8 6.0 %collective-permute-start.4 = (bf16[32,6,6,1]{3,2,1,0:T(8,128)(2,1)}, bf16[32,6,6,1]{3,2,1,0:T(8,128)(2,1)}, u32[]{:S(2)}, u32[]{:S(2)}) collective-permute-start(bf16[32,6,6,1]{3,2,1,0:T(8,128)(2,1)} %get-tuple-element.112), channel_id=1, source_target_pairs={{0,1},{1,2},{2,3},{4,5},{5,6},{6,7},{8,9},{9,10},{10,11},{12,13},{... | collective-permute-start | bytes 6920 | tf_op jit(solution)/shard_map/ppermute | solution.py:15
  40.0 9.7 %collective-permute-done.5 = bf16[32,6,6,1]{3,2,1,0:T(8,128)(2,1)} collective-permute-done((bf16[32,6,6,1]{3,2,1,0:T(8,128)(2,1)}, bf16[32,6,6,1]{3,2,1,0:T(8,128)(2,1)}, u32[]{:S(2)}, u32[]{:S(2)}) %collective-permute-start.5) | collective-permute-done | bytes 2336 | tf_op jit(solution)/shard_map/ppermute | solution.py:17
  50.2 3.7 pad_maximum_fusion.2
  54.0 4.1 fusion.339
  99.3 4.5 collective-permute-start.7
  106.6 3.4 collective-permute-start.8
  114.6 4.1 collective-permute-done.9
  120.5 5.6 %collective-permute-start.10 = (bf16[32,6,6,1]{3,2,1,0:T(8,128)(2,1)}, bf16[32,6,6,1]{3,2,1,0:T(8,128)(2,1)}, u32[]{:S(2)}, u32[]{:S(2)}) collective-permute-start(bf16[32,6,6,1]{3,2,1,0:T(8,128)(2,1)} %get-tuple-element.107), channel_id=1, source_target_pairs={{0,1},{1,2},{2,3},{4,5},{5,6},{6,7},{8,9},{9,10},{10,11},{12,13},{... | collective-permute-start | bytes 6920 | tf_op jit(solution)/shard_map/ppermute | solution.py:15
  141.3 6.6 %collective-permute-done.11 = bf16[32,6,6,1]{3,2,1,0:T(8,128)(2,1)} collective-permute-done((bf16[32,6,6,1]{3,2,1,0:T(8,128)(2,1)}, bf16[32,6,6,1]{3,2,1,0:T(8,128)(2,1)}, u32[]{:S(2)}, u32[]{:S(2)}) %collective-permute-start.11) | collective-permute-done | bytes 2336 | tf_op jit(solution)/shard_map/ppermute | solution.py:17
  147.9 4.1 maximum_maximum_fusion.3
  175.6 3.4 fusion.338
  205.8 4.5 collective-permute-start.13
  212.4 3.1 collective-permute-start.14
  217.1 4.2 collective-permute-done.15
  221.4 3.2 collective-permute-start.16
  224.7 3.5 collective-permute-start.17
  229.3 5.0 %collective-permute-done.17 = bf16[32,4,4,1]{3,0,2,1:T(8,128)(2,1)S(1)} collective-permute-done((bf16[32,4,4,1]{3,0,2,1:T(8,128)(2,1)S(1)}, bf16[32,4,4,1]{3,0,2,1:T(8,128)(2,1)S(1)}, u32[]{:S(2)}, u32[]{:S(2)}) %collective-permute-start.17) | collective-permute-done | bytes 1056 | tf_op jit(solution)/shard_map/ppermute | solution.py:17
  242.2 4.5 collective-permute-start.19
  248.8 2.5 collective-permute-start.20
  254.4 4.1 collective-permute-done.21
  261.9 5.1 %collective-permute-start.23 = (bf16[64,4,4,1]{3,2,1,0:T(4,128)(2,1)S(1)}, bf16[64,4,4,1]{3,2,1,0:T(4,128)(2,1)S(1)}, u32[]{:S(2)}, u32[]{:S(2)}) collective-permute-start(bf16[64,4,4,1]{3,2,1,0:T(4,128)(2,1)S(1)} %get-tuple-element.170), channel_id=1, source_target_pairs={{1,0},{2,1},{3,2},{5,4},{6,5},{7,6},{9,8},{10,9},{11,10},{13,12},{... | collective-permute-start | bytes 6152 | tf_op jit(solution)/shard_map/ppermute | solution.py:17
  270.8 7.8 %collective-permute-done.23 = bf16[64,4,4,1]{3,2,1,0:T(4,128)(2,1)S(1)} collective-permute-done((bf16[64,4,4,1]{3,2,1,0:T(4,128)(2,1)S(1)}, bf16[64,4,4,1]{3,2,1,0:T(4,128)(2,1)S(1)}, u32[]{:S(2)}, u32[]{:S(2)}) %collective-permute-start.23) | collective-permute-done | bytes 2080 | tf_op jit(solution)/shard_map/ppermute | solution.py:17
  298.9 4.2 all-to-all-start
  323.2 4.8 collective-permute-start.25
  332.2 8.4 %all-to-all-start.1 = ((bf16[64,1,64]{2,1,0:T(2,128)(2,1)}), bf16[64,1,64]{2,1,0:T(2,128)(2,1)S(1)}, u32[]{:S(2)}, u32[]{:S(2)}) async-start(bf16[64,1,64]{2,1,0:T(2,128)(2,1)} %copy.374), calls=%async_computation.1 | async-start | bytes 65536 | tf_op jit(solution)/shard_map/all_to_all | solution.py:118
  340.6 7.0 %all-to-all-done.1 = bf16[64,1,64]{2,1,0:T(2,128)(2,1)S(1)} async-done(((bf16[64,1,64]{2,1,0:T(2,128)(2,1)}), bf16[64,1,64]{2,1,0:T(2,128)(2,1)S(1)}, u32[]{:S(2)}, u32[]{:S(2)}) %all-to-all-start.1) | async-done | bytes 8224 | tf_op jit(solution)/shard_map/all_to_all | solution.py:118
  348.5 5.6 %all-to-all-start.2 = ((bf16[1,128,64]{2,0,1:T(2,128)(2,1)}), bf16[1,128,64]{2,0,1:T(2,128)(2,1)S(1)}, u32[]{:S(2)}, u32[]{:S(2)}) async-start(bf16[1,128,64]{2,0,1:T(2,128)(2,1)} %copy.375), calls=%async_computation.2 | async-start | bytes 131072 | tf_op jit(solution)/shard_map/all_to_all | solution.py:103
  354.3 7.0 %all-to-all-done.2 = bf16[1,128,64]{2,0,1:T(2,128)(2,1)S(1)} async-done(((bf16[1,128,64]{2,0,1:T(2,128)(2,1)}), bf16[1,128,64]{2,0,1:T(2,128)(2,1)S(1)}, u32[]{:S(2)}, u32[]{:S(2)}) %all-to-all-start.2) | async-done | bytes 16416 | tf_op jit(solution)/shard_map/all_to_all | solution.py:103
  363.3 4.8 collective-permute-start.27
  368.2 3.3 collective-permute-done.27
  372.2 12.2 %all_to_all.16 = bf16[64,2,64]{2,1,0:T(2,128)(2,1)S(1)} all-to-all(bf16[64,2,64]{2,1,0:T(2,128)(2,1)S(1)} %copy.378), channel_id=1, replica_groups=mesh['gx'=16,'gy'=4,'gz'=4] {'gx','gy'}, dimensions={0} | all-to-all | bytes 32768 | tf_op jit(solution)/shard_map/all_to_all | solution.py:118
  386.6 4.5 collective-permute-start.29
  393.8 2.5 collective-permute-start.30
  397.9 4.2 collective-permute-done.30
  402.2 4.1 collective-permute-done.31
  406.4 3.7 collective-permute-start.33
  410.0 4.3 collective-permute-start.32
  427.0 4.5 collective-permute-start.35
  431.6 3.0 collective-permute-done.34
  435.8 2.5 collective-permute-start.36
  441.1 5.6 %collective-permute-done.36 = bf16[96,6,1,256]{0,3,2,1:T(8,128)(2,1)S(1)} collective-permute-done((bf16[96,6,1,256]{0,3,2,1:T(8,128)(2,1)S(1)}, bf16[96,6,1,256]{0,3,2,1:T(8,128)(2,1)S(1)}, u32[]{:S(2)}, u32[]{:S(2)}) %collective-permute-start.36) | collective-permute-done | bytes 294944 | tf_op jit(solution)/shard_map/ppermute | solution.py:15
  446.7 4.3 collective-permute-done.37
  451.1 5.5 %collective-permute-start.38 = (bf16[96,6,6,1]{0,3,2,1:T(2,128)(2,1)S(1)}, bf16[96,6,6,1]{0,3,2,1:T(2,128)(2,1)S(1)}, u32[]{:S(2)}, u32[]{:S(2)}) collective-permute-start(bf16[96,6,6,1]{0,3,2,1:T(2,128)(2,1)S(1)} %get-tuple-element.7), channel_id=1, source_target_pairs={{0,1},{1,2},{2,3},{4,5},{5,6},{6,7},{8,9},{9,10},{10,11},{12,13},{... | collective-permute-start | bytes 20744 | tf_op jit(solution)/shard_map/ppermute | solution.py:15
  464.4 4.2 maximum_maximum_fusion
  471.3 3.4 fusion.334
  (557 shorter events, 236.8 us)
Async XLA Ops:
  0.0 384.4 %copy-start = (bf16[128,128]{1,0:T(8,128)(2,1)S(1)}, bf16[128,128]{1,0:T(8,128)(2,1)}, u32[]{:S(2)}) copy-start(bf16[128,128]{1,0:T(8,128)(2,1)} %param.19) | copy-start | bytes 98308
  0.0 15.8 %copy-start.14 = (bf16[32,4,4,256]{3,2,1,0:T(4,128)(2,1)S(1)}, bf16[32,4,4,256]{3,2,1,0:T(4,128)(2,1)}, u32[]{:S(2)}) copy-start(bf16[32,4,4,256]{3,2,1,0:T(4,128)(2,1)} %param.11) | copy-start | bytes 786436
  1.0 6.5 %collective-permute-start = (bf16[32,1,4,256]{3,2,1,0:T(4,128)(2,1)S(1)}, bf16[32,1,4,256]{3,2,1,0:T(4,128)(2,1)S(1)}, u32[]{:S(2)}, u32[]{:S(2)}) collective-permute-start(bf16[32,1,4,256]{3,2,1,0:T(4,128)(2,1)S(1)} %get-tuple-element.198), channel_id=1, source_target_pairs={{0,16},{16,32},{32,48},{48,64},{64,80},{80,96},{96,112},{112,128},... | collective-permute-start | bytes 196616 | tf_op jit(solution)/shard_map/ppermute | solution.py:15
  2.9 6.4 %collective-permute-start.1 = (bf16[32,1,4,256]{3,2,1,0:T(4,128)(2,1)S(1)}, bf16[32,1,4,256]{3,2,1,0:T(4,128)(2,1)S(1)}, u32[]{:S(2)}, u32[]{:S(2)}) collective-permute-start(bf16[32,1,4,256]{3,2,1,0:T(4,128)(2,1)S(1)} %get-tuple-element.197), channel_id=1, source_target_pairs={{16,0},{32,16},{48,32},{64,48},{80,64},{96,80},{112,96},{128,112},... | collective-permute-start | bytes 196616 | tf_op jit(solution)/shard_map/ppermute | solution.py:17
  11.1 8.5 %collective-permute-start.2 = (bf16[32,6,1,256]{3,2,1,0:T(2,128)(2,1)S(1)}, bf16[32,6,1,256]{3,2,1,0:T(2,128)(2,1)S(1)}, u32[]{:S(2)}, u32[]{:S(2)}) collective-permute-start(bf16[32,6,1,256]{3,2,1,0:T(2,128)(2,1)S(1)} %get-tuple-element.157), channel_id=1, source_target_pairs={{0,4},{4,8},{8,12},{1,5},{5,9},{9,13},{2,6},{6,10},{10,14},{3,7},{... | collective-permute-start | bytes 294920 | tf_op jit(solution)/shard_map/ppermute | solution.py:15
  14.5 9.6 %collective-permute-start.3 = (bf16[32,6,1,256]{3,2,1,0:T(2,128)(2,1)S(1)}, bf16[32,6,1,256]{3,2,1,0:T(2,128)(2,1)S(1)}, u32[]{:S(2)}, u32[]{:S(2)}) collective-permute-start(bf16[32,6,1,256]{3,2,1,0:T(2,128)(2,1)S(1)} %get-tuple-element.158), channel_id=1, source_target_pairs={{4,0},{8,4},{12,8},{5,1},{9,5},{13,9},{6,2},{10,6},{14,10},{7,3},{... | collective-permute-start | bytes 294920 | tf_op jit(solution)/shard_map/ppermute | solution.py:17
  25.9 23.8 %collective-permute-start.5 = (bf16[32,6,6,1]{3,2,1,0:T(8,128)(2,1)}, bf16[32,6,6,1]{3,2,1,0:T(8,128)(2,1)}, u32[]{:S(2)}, u32[]{:S(2)}) collective-permute-start(bf16[32,6,6,1]{3,2,1,0:T(8,128)(2,1)} %get-tuple-element.111), channel_id=1, source_target_pairs={{1,0},{2,1},{3,2},{5,4},{6,5},{7,6},{9,8},{10,9},{11,10},{13,12},{... | collective-permute-start | bytes 6920 | tf_op jit(solution)/shard_map/ppermute | solution.py:17
  27.8 22.5 %collective-permute-start.4 = (bf16[32,6,6,1]{3,2,1,0:T(8,128)(2,1)}, bf16[32,6,6,1]{3,2,1,0:T(8,128)(2,1)}, u32[]{:S(2)}, u32[]{:S(2)}) collective-permute-start(bf16[32,6,6,1]{3,2,1,0:T(8,128)(2,1)} %get-tuple-element.112), channel_id=1, source_target_pairs={{0,1},{1,2},{2,3},{4,5},{5,6},{6,7},{8,9},{9,10},{10,11},{12,13},{... | collective-permute-start | bytes 6920 | tf_op jit(solution)/shard_map/ppermute | solution.py:15
  97.3 6.7 %collective-permute-start.6 = (bf16[32,1,4,256]{3,2,1,0:T(4,128)(2,1)S(1)}, bf16[32,1,4,256]{3,2,1,0:T(4,128)(2,1)S(1)}, u32[]{:S(2)}, u32[]{:S(2)}) collective-permute-start(bf16[32,1,4,256]{3,2,1,0:T(4,128)(2,1)S(1)} %get-tuple-element.193), channel_id=1, source_target_pairs={{0,16},{16,32},{32,48},{48,64},{64,80},{80,96},{96,112},{112,128},... | collective-permute-start | bytes 196616 | tf_op jit(solution)/shard_map/ppermute | solution.py:15
  99.3 6.4 %collective-permute-start.7 = (bf16[32,1,4,256]{3,2,1,0:T(4,128)(2,1)S(1)}, bf16[32,1,4,256]{3,2,1,0:T(4,128)(2,1)S(1)}, u32[]{:S(2)}, u32[]{:S(2)}) collective-permute-start(bf16[32,1,4,256]{3,2,1,0:T(4,128)(2,1)S(1)} %get-tuple-element.192), channel_id=1, source_target_pairs={{16,0},{32,16},{48,32},{64,48},{80,64},{96,80},{112,96},{128,112},... | collective-permute-start | bytes 196616 | tf_op jit(solution)/shard_map/ppermute | solution.py:17
  106.6 8.1 %collective-permute-start.8 = (bf16[32,6,1,256]{3,2,1,0:T(2,128)(2,1)S(1)}, bf16[32,6,1,256]{3,2,1,0:T(2,128)(2,1)S(1)}, u32[]{:S(2)}, u32[]{:S(2)}) collective-permute-start(bf16[32,6,1,256]{3,2,1,0:T(2,128)(2,1)S(1)} %get-tuple-element.152), channel_id=1, source_target_pairs={{0,4},{4,8},{8,12},{1,5},{5,9},{9,13},{2,6},{6,10},{10,14},{3,7},{... | collective-permute-start | bytes 294920 | tf_op jit(solution)/shard_map/ppermute | solution.py:15
  110.0 8.8 %collective-permute-start.9 = (bf16[32,6,1,256]{3,2,1,0:T(2,128)(2,1)S(1)}, bf16[32,6,1,256]{3,2,1,0:T(2,128)(2,1)S(1)}, u32[]{:S(2)}, u32[]{:S(2)}) collective-permute-start(bf16[32,6,1,256]{3,2,1,0:T(2,128)(2,1)S(1)} %get-tuple-element.153), channel_id=1, source_target_pairs={{4,0},{8,4},{12,8},{5,1},{9,5},{13,9},{6,2},{10,6},{14,10},{7,3},{... | collective-permute-start | bytes 294920 | tf_op jit(solution)/shard_map/ppermute | solution.py:17
  120.5 20.8 %collective-permute-start.10 = (bf16[32,6,6,1]{3,2,1,0:T(8,128)(2,1)}, bf16[32,6,6,1]{3,2,1,0:T(8,128)(2,1)}, u32[]{:S(2)}, u32[]{:S(2)}) collective-permute-start(bf16[32,6,6,1]{3,2,1,0:T(8,128)(2,1)} %get-tuple-element.107), channel_id=1, source_target_pairs={{0,1},{1,2},{2,3},{4,5},{5,6},{6,7},{8,9},{9,10},{10,11},{12,13},{... | collective-permute-start | bytes 6920 | tf_op jit(solution)/shard_map/ppermute | solution.py:15
  126.1 21.8 %collective-permute-start.11 = (bf16[32,6,6,1]{3,2,1,0:T(8,128)(2,1)}, bf16[32,6,6,1]{3,2,1,0:T(8,128)(2,1)}, u32[]{:S(2)}, u32[]{:S(2)}) collective-permute-start(bf16[32,6,6,1]{3,2,1,0:T(8,128)(2,1)} %get-tuple-element.108), channel_id=1, source_target_pairs={{1,0},{2,1},{3,2},{5,4},{6,5},{7,6},{9,8},{10,9},{11,10},{13,12},{... | collective-permute-start | bytes 6920 | tf_op jit(solution)/shard_map/ppermute | solution.py:17
  203.9 6.6 %collective-permute-start.12 = (bf16[32,1,2,128]{0,3,2,1:T(8,128)(2,1)S(1)}, bf16[32,1,2,128]{0,3,2,1:T(8,128)(2,1)S(1)}, u32[]{:S(2)}, u32[]{:S(2)}) collective-permute-start(bf16[32,1,2,128]{0,3,2,1:T(8,128)(2,1)S(1)} %get-tuple-element.208), channel_id=1, source_target_pairs={{0,16},{16,32},{32,48},{48,64},{64,80},{80,96},{96,112},{112,128},... | collective-permute-start | bytes 49160 | tf_op jit(solution)/shard_map/ppermute | solution.py:15
  205.8 6.4 %collective-permute-start.13 = (bf16[32,1,2,128]{0,3,2,1:T(8,128)(2,1)S(1)}, bf16[32,1,2,128]{0,3,2,1:T(8,128)(2,1)S(1)}, u32[]{:S(2)}, u32[]{:S(2)}) collective-permute-start(bf16[32,1,2,128]{0,3,2,1:T(8,128)(2,1)S(1)} %get-tuple-element.209), channel_id=1, source_target_pairs={{16,0},{32,16},{48,32},{64,48},{80,64},{96,80},{112,96},{128,112},... | collective-permute-start | bytes 49160 | tf_op jit(solution)/shard_map/ppermute | solution.py:17
  212.4 4.7 collective-permute-start.14
  215.5 5.8 %collective-permute-start.15 = (bf16[32,4,1,128]{3,0,2,1:T(8,128)(2,1)S(1)}, bf16[32,4,1,128]{3,0,2,1:T(8,128)(2,1)S(1)}, u32[]{:S(2)}, u32[]{:S(2)}) collective-permute-start(bf16[32,4,1,128]{3,0,2,1:T(8,128)(2,1)S(1)} %get-tuple-element.224), channel_id=1, source_target_pairs={{4,0},{8,4},{12,8},{5,1},{9,5},{13,9},{6,2},{10,6},{14,10},{7,3},{... | collective-permute-start | bytes 98312 | tf_op jit(solution)/shard_map/ppermute | solution.py:17
  221.4 7.9 %collective-permute-start.16 = (bf16[32,4,4,1]{3,0,2,1:T(8,128)(2,1)S(1)}, bf16[32,4,4,1]{3,0,2,1:T(8,128)(2,1)S(1)}, u32[]{:S(2)}, u32[]{:S(2)}) collective-permute-start(bf16[32,4,4,1]{3,0,2,1:T(8,128)(2,1)S(1)} %get-tuple-element.206), channel_id=1, source_target_pairs={{0,1},{1,2},{2,3},{4,5},{5,6},{6,7},{8,9},{9,10},{10,11},{12,13},{... | collective-permute-start | bytes 3080 | tf_op jit(solution)/shard_map/ppermute | solution.py:15
  224.7 9.6 %collective-permute-start.17 = (bf16[32,4,4,1]{3,0,2,1:T(8,128)(2,1)S(1)}, bf16[32,4,4,1]{3,0,2,1:T(8,128)(2,1)S(1)}, u32[]{:S(2)}, u32[]{:S(2)}) collective-permute-start(bf16[32,4,4,1]{3,0,2,1:T(8,128)(2,1)S(1)} %get-tuple-element.207), channel_id=1, source_target_pairs={{1,0},{2,1},{3,2},{5,4},{6,5},{7,6},{9,8},{10,9},{11,10},{13,12},{... | collective-permute-start | bytes 3080 | tf_op jit(solution)/shard_map/ppermute | solution.py:17
  240.3 6.5 %collective-permute-start.18 = (bf16[64,1,2,128]{3,2,1,0:T(2,128)(2,1)S(1)}, bf16[64,1,2,128]{3,2,1,0:T(2,128)(2,1)S(1)}, u32[]{:S(2)}, u32[]{:S(2)}) collective-permute-start(bf16[64,1,2,128]{3,2,1,0:T(2,128)(2,1)S(1)} %get-tuple-element.220), channel_id=1, source_target_pairs={{0,16},{16,32},{32,48},{48,64},{64,80},{80,96},{96,112},{112,128},... | collective-permute-start | bytes 98312 | tf_op jit(solution)/shard_map/ppermute | solution.py:15
  242.2 6.1 %collective-permute-start.19 = (bf16[64,1,2,128]{3,2,1,0:T(2,128)(2,1)S(1)}, bf16[64,1,2,128]{3,2,1,0:T(2,128)(2,1)S(1)}, u32[]{:S(2)}, u32[]{:S(2)}) collective-permute-start(bf16[64,1,2,128]{3,2,1,0:T(2,128)(2,1)S(1)} %get-tuple-element.219), channel_id=1, source_target_pairs={{16,0},{32,16},{48,32},{64,48},{80,64},{96,80},{112,96},{128,112},... | collective-permute-start | bytes 98312 | tf_op jit(solution)/shard_map/ppermute | solution.py:17
  248.8 5.5 %collective-permute-start.20 = (bf16[64,4,1,128]{3,2,1,0:T(2,128)(2,1)S(1)}, bf16[64,4,1,128]{3,2,1,0:T(2,128)(2,1)S(1)}, u32[]{:S(2)}, u32[]{:S(2)}) collective-permute-start(bf16[64,4,1,128]{3,2,1,0:T(2,128)(2,1)S(1)} %get-tuple-element.202), channel_id=1, source_target_pairs={{0,4},{4,8},{8,12},{1,5},{5,9},{9,13},{2,6},{6,10},{10,14},{3,7},{... | collective-permute-start | bytes 196616 | tf_op jit(solution)/shard_map/ppermute | solution.py:15
  251.4 7.1 %collective-permute-start.21 = (bf16[64,4,1,128]{3,2,1,0:T(2,128)(2,1)S(1)}, bf16[64,4,1,128]{3,2,1,0:T(2,128)(2,1)S(1)}, u32[]{:S(2)}, u32[]{:S(2)}) collective-permute-start(bf16[64,4,1,128]{3,2,1,0:T(2,128)(2,1)S(1)} %get-tuple-element.203), channel_id=1, source_target_pairs={{4,0},{8,4},{12,8},{5,1},{9,5},{13,9},{6,2},{10,6},{14,10},{7,3},{... | collective-permute-start | bytes 196616 | tf_op jit(solution)/shard_map/ppermute | solution.py:17
  259.8 11.0 %collective-permute-start.22 = (bf16[64,4,4,1]{3,2,1,0:T(4,128)(2,1)}, bf16[64,4,4,1]{3,2,1,0:T(4,128)(2,1)S(1)}, u32[]{:S(2)}, u32[]{:S(2)}) collective-permute-start(bf16[64,4,4,1]{3,2,1,0:T(4,128)(2,1)} %get-tuple-element.169), channel_id=1, source_target_pairs={{0,1},{1,2},{2,3},{4,5},{5,6},{6,7},{8,9},{9,10},{10,11},{12,13},{... | collective-permute-start | bytes 6152 | tf_op jit(solution)/shard_map/ppermute | solution.py:15
  261.9 16.8 %collective-permute-start.23 = (bf16[64,4,4,1]{3,2,1,0:T(4,128)(2,1)S(1)}, bf16[64,4,4,1]{3,2,1,0:T(4,128)(2,1)S(1)}, u32[]{:S(2)}, u32[]{:S(2)}) collective-permute-start(bf16[64,4,4,1]{3,2,1,0:T(4,128)(2,1)S(1)} %get-tuple-element.170), channel_id=1, source_target_pairs={{1,0},{2,1},{3,2},{5,4},{6,5},{7,6},{9,8},{10,9},{11,10},{13,12},{... | collective-permute-start | bytes 6152 | tf_op jit(solution)/shard_map/ppermute | solution.py:17
  296.0 51.6 %copy-start.60 = (bf16[128,64]{0,1:T(8,128)(2,1)S(1)}, bf16[128,64]{0,1:T(8,128)(2,1)}, u32[]{:S(2)}) copy-start(bf16[128,64]{0,1:T(8,128)(2,1)} %param.17) | copy-start | bytes 49156
  296.3 57.9 %copy-start.59 = (bf16[128,27]{0,1:T(8,128)(2,1)S(1)}, bf16[128,27]{0,1:T(8,128)(2,1)}, u32[]{:S(2)}) copy-start(bf16[128,27]{0,1:T(8,128)(2,1)} %param.18) | copy-start | bytes 20740
  297.9 93.3 %copy-start.15 = (bf16[64,5184]{1,0:T(8,128)(2,1)S(1)}, bf16[64,5184]{1,0:T(8,128)(2,1)}, u32[]{:S(2)}) copy-start(bf16[64,5184]{1,0:T(8,128)(2,1)} %param.20) | copy-start | bytes 1990660
  298.9 22.3 %all-to-all-start = ((bf16[1,64,64]{2,0,1:T(2,128)(2,1)}), bf16[1,64,64]{2,0,1:T(2,128)(2,1)S(1)}, u32[]{:S(2)}, u32[]{:S(2)}) async-start(bf16[1,64,64]{2,0,1:T(2,128)(2,1)} %copy.373), calls=%async_computation | async-start | bytes 65536 | tf_op jit(solution)/shard_map/all_to_all | solution.py:103
  321.3 7.4 %collective-permute-start.24 = (bf16[1,16,4,1]{3,2,1,0:T(4,128)(2,1)S(1)}, bf16[1,16,4,1]{3,2,1,0:T(4,128)(2,1)S(1)}, u32[]{:S(2)}, u32[]{:S(2)}) collective-permute-start(bf16[1,16,4,1]{3,2,1,0:T(4,128)(2,1)S(1)} %get-tuple-element.229), channel_id=1, source_target_pairs={{0,1},{1,2},{2,3},{4,5},{5,6},{6,7},{8,9},{9,10},{10,11},{12,13},{... | collective-permute-start | bytes 392 | tf_op jit(solution)/shard_map/ppermute | solution.py:15
  323.2 7.8 %collective-permute-start.25 = (bf16[1,16,4,1]{3,2,1,0:T(4,128)(2,1)S(1)}, bf16[1,16,4,1]{3,2,1,0:T(4,128)(2,1)S(1)}, u32[]{:S(2)}, u32[]{:S(2)}) collective-permute-start(bf16[1,16,4,1]{3,2,1,0:T(4,128)(2,1)S(1)} %get-tuple-element.230), channel_id=1, source_target_pairs={{1,0},{2,1},{3,2},{5,4},{6,5},{7,6},{9,8},{10,9},{11,10},{13,12},{... | collective-permute-start | bytes 392 | tf_op jit(solution)/shard_map/ppermute | solution.py:17
  332.2 15.4 %all-to-all-start.1 = ((bf16[64,1,64]{2,1,0:T(2,128)(2,1)}), bf16[64,1,64]{2,1,0:T(2,128)(2,1)S(1)}, u32[]{:S(2)}, u32[]{:S(2)}) async-start(bf16[64,1,64]{2,1,0:T(2,128)(2,1)} %copy.374), calls=%async_computation.1 | async-start | bytes 65536 | tf_op jit(solution)/shard_map/all_to_all | solution.py:118
  348.5 12.7 %all-to-all-start.2 = ((bf16[1,128,64]{2,0,1:T(2,128)(2,1)}), bf16[1,128,64]{2,0,1:T(2,128)(2,1)S(1)}, u32[]{:S(2)}, u32[]{:S(2)}) async-start(bf16[1,128,64]{2,0,1:T(2,128)(2,1)} %copy.375), calls=%async_computation.2 | async-start | bytes 131072 | tf_op jit(solution)/shard_map/all_to_all | solution.py:103
  361.4 6.9 %collective-permute-start.26 = (bf16[2,16,4,1]{3,1,2,0:T(8,128)(2,1)S(1)}, bf16[2,16,4,1]{3,1,2,0:T(8,128)(2,1)S(1)}, u32[]{:S(2)}, u32[]{:S(2)}) collective-permute-start(bf16[2,16,4,1]{3,1,2,0:T(8,128)(2,1)S(1)} %get-tuple-element.225), channel_id=1, source_target_pairs={{0,1},{1,2},{2,3},{4,5},{5,6},{6,7},{8,9},{9,10},{10,11},{12,13},{... | collective-permute-start | bytes 776 | tf_op jit(solution)/shard_map/ppermute | solution.py:15
  363.3 8.3 %collective-permute-start.27 = (bf16[2,16,4,1]{3,1,2,0:T(8,128)(2,1)S(1)}, bf16[2,16,4,1]{3,1,2,0:T(8,128)(2,1)S(1)}, u32[]{:S(2)}, u32[]{:S(2)}) collective-permute-start(bf16[2,16,4,1]{3,1,2,0:T(8,128)(2,1)S(1)} %get-tuple-element.226), channel_id=1, source_target_pairs={{1,0},{2,1},{3,2},{5,4},{6,5},{7,6},{9,8},{10,9},{11,10},{13,12},{... | collective-permute-start | bytes 776 | tf_op jit(solution)/shard_map/ppermute | solution.py:17
  384.7 7.2 %collective-permute-start.28 = (bf16[192,1,2,128]{0,3,2,1:T(8,128)(2,1)S(1)}, bf16[192,1,2,128]{0,3,2,1:T(8,128)(2,1)S(1)}, u32[]{:S(2)}, u32[]{:S(2)}) collective-permute-start(bf16[192,1,2,128]{0,3,2,1:T(8,128)(2,1)S(1)} %get-tuple-element.161), channel_id=1, source_target_pairs={{0,16},{16,32},{32,48},{48,64},{64,80},{80,96},{96,112},{112,128},... | collective-permute-start | bytes 294920 | tf_op jit(solution)/shard_map/ppermute | solution.py:15
  386.6 7.0 %collective-permute-start.29 = (bf16[192,1,2,128]{0,3,2,1:T(8,128)(2,1)S(1)}, bf16[192,1,2,128]{0,3,2,1:T(8,128)(2,1)S(1)}, u32[]{:S(2)}, u32[]{:S(2)}) collective-permute-start(bf16[192,1,2,128]{0,3,2,1:T(8,128)(2,1)S(1)} %get-tuple-element.162), channel_id=1, source_target_pairs={{16,0},{32,16},{48,32},{64,48},{80,64},{96,80},{112,96},{128,112},... | collective-permute-start | bytes 294920 | tf_op jit(solution)/shard_map/ppermute | solution.py:17
  393.8 8.3 %collective-permute-start.30 = (bf16[192,4,1,128]{0,3,2,1:T(8,128)(2,1)S(1)}, bf16[192,4,1,128]{0,3,2,1:T(8,128)(2,1)S(1)}, u32[]{:S(2)}, u32[]{:S(2)}) collective-permute-start(bf16[192,4,1,128]{0,3,2,1:T(8,128)(2,1)S(1)} %get-tuple-element.127), channel_id=1, source_target_pairs={{0,4},{4,8},{8,12},{1,5},{5,9},{9,13},{2,6},{6,10},{10,14},{3,7},{... | collective-permute-start | bytes 589832 | tf_op jit(solution)/shard_map/ppermute | solution.py:15
  396.3 10.0 %collective-permute-start.31 = (bf16[192,4,1,128]{0,3,2,1:T(8,128)(2,1)S(1)}, bf16[192,4,1,128]{0,3,2,1:T(8,128)(2,1)S(1)}, u32[]{:S(2)}, u32[]{:S(2)}) collective-permute-start(bf16[192,4,1,128]{0,3,2,1:T(8,128)(2,1)S(1)} %get-tuple-element.128), channel_id=1, source_target_pairs={{4,0},{8,4},{12,8},{5,1},{9,5},{13,9},{6,2},{10,6},{14,10},{7,3},{... | collective-permute-start | bytes 589832 | tf_op jit(solution)/shard_map/ppermute | solution.py:17
  406.4 8.6 %collective-permute-start.33 = (bf16[192,4,4,1]{0,2,3,1:T(4,128)(2,1)S(1)}, bf16[192,4,4,1]{0,2,3,1:T(4,128)(2,1)S(1)}, u32[]{:S(2)}, u32[]{:S(2)}) collective-permute-start(bf16[192,4,4,1]{0,2,3,1:T(4,128)(2,1)S(1)} %copy.384), channel_id=1, source_target_pairs={{1,0},{2,1},{3,2},{5,4},{6,5},{7,6},{9,8},{10,9},{11,10},{13,12},{... | collective-permute-start | bytes 18440 | tf_op jit(solution)/shard_map/ppermute | solution.py:17
  410.0 6.4 %collective-permute-start.32 = (bf16[192,4,4,1]{0,2,3,1:T(4,128)(2,1)S(1)}, bf16[192,4,4,1]{0,2,3,1:T(4,128)(2,1)S(1)}, u32[]{:S(2)}, u32[]{:S(2)}) collective-permute-start(bf16[192,4,4,1]{0,2,3,1:T(4,128)(2,1)S(1)} %copy.380), channel_id=1, source_target_pairs={{0,1},{1,2},{2,3},{4,5},{5,6},{6,7},{8,9},{9,10},{10,11},{12,13},{... | collective-permute-start | bytes 18440 | tf_op jit(solution)/shard_map/ppermute | solution.py:15
  425.1 9.5 %collective-permute-start.34 = (bf16[96,1,4,256]{0,3,2,1:T(8,128)(2,1)S(1)}, bf16[96,1,4,256]{0,3,2,1:T(8,128)(2,1)S(1)}, u32[]{:S(2)}, u32[]{:S(2)}) collective-permute-start(bf16[96,1,4,256]{0,3,2,1:T(8,128)(2,1)S(1)} %get-tuple-element.33), channel_id=1, source_target_pairs={{0,16},{16,32},{32,48},{48,64},{64,80},{80,96},{96,112},{112,128},... | collective-permute-start | bytes 589832 | tf_op jit(solution)/shard_map/ppermute | solution.py:15
  427.0 8.4 %collective-permute-start.35 = (bf16[96,1,4,256]{0,3,2,1:T(8,128)(2,1)S(1)}, bf16[96,1,4,256]{0,3,2,1:T(8,128)(2,1)S(1)}, u32[]{:S(2)}, u32[]{:S(2)}) collective-permute-start(bf16[96,1,4,256]{0,3,2,1:T(8,128)(2,1)S(1)} %get-tuple-element.34), channel_id=1, source_target_pairs={{16,0},{32,16},{48,32},{64,48},{80,64},{96,80},{112,96},{128,112},... | collective-permute-start | bytes 589832 | tf_op jit(solution)/shard_map/ppermute | solution.py:17
  435.8 10.9 %collective-permute-start.36 = (bf16[96,6,1,256]{0,3,2,1:T(8,128)(2,1)S(1)}, bf16[96,6,1,256]{0,3,2,1:T(8,128)(2,1)S(1)}, u32[]{:S(2)}, u32[]{:S(2)}) collective-permute-start(bf16[96,6,1,256]{0,3,2,1:T(8,128)(2,1)S(1)} %get-tuple-element.11), channel_id=1, source_target_pairs={{0,4},{4,8},{8,12},{1,5},{5,9},{9,13},{2,6},{6,10},{10,14},{3,7},{... | collective-permute-start | bytes 884744 | tf_op jit(solution)/shard_map/ppermute | solution.py:15
  438.3 12.6 %collective-permute-start.37 = (bf16[96,6,1,256]{0,3,2,1:T(8,128)(2,1)S(1)}, bf16[96,6,1,256]{0,3,2,1:T(8,128)(2,1)S(1)}, u32[]{:S(2)}, u32[]{:S(2)}) collective-permute-start(bf16[96,6,1,256]{0,3,2,1:T(8,128)(2,1)S(1)} %get-tuple-element.12), channel_id=1, source_target_pairs={{4,0},{8,4},{12,8},{5,1},{9,5},{13,9},{6,2},{10,6},{14,10},{7,3},{... | collective-permute-start | bytes 884744 | tf_op jit(solution)/shard_map/ppermute | solution.py:17
  451.1 12.3 %collective-permute-start.38 = (bf16[96,6,6,1]{0,3,2,1:T(2,128)(2,1)S(1)}, bf16[96,6,6,1]{0,3,2,1:T(2,128)(2,1)S(1)}, u32[]{:S(2)}, u32[]{:S(2)}) collective-permute-start(bf16[96,6,6,1]{0,3,2,1:T(2,128)(2,1)S(1)} %get-tuple-element.7), channel_id=1, source_target_pairs={{0,1},{1,2},{2,3},{4,5},{5,6},{6,7},{8,9},{9,10},{10,11},{12,13},{... | collective-permute-start | bytes 20744 | tf_op jit(solution)/shard_map/ppermute | solution.py:15
  456.6 7.8 %collective-permute-start.39 = (bf16[96,6,6,1]{0,3,2,1:T(2,128)(2,1)S(1)}, bf16[96,6,6,1]{0,3,2,1:T(2,128)(2,1)S(1)}, u32[]{:S(2)}, u32[]{:S(2)}) collective-permute-start(bf16[96,6,6,1]{0,3,2,1:T(2,128)(2,1)S(1)} %get-tuple-element.8), channel_id=1, source_target_pairs={{1,0},{2,1},{3,2},{5,4},{6,5},{7,6},{9,8},{10,9},{11,10},{13,12},{... | collective-permute-start | bytes 20744 | tf_op jit(solution)/shard_map/ppermute | solution.py:17
  (56 other events, 214.4 us)
where the time goes:
time: 496 us; the launch traced here: 486 us
  starting transfers between devices  141 us (28%)
  waiting for transfers between devices  106 us (21%)
  local copies, waits for them, and re-layouts  104 us (21%)
  matrix products  71.7 us (14%)
  other arithmetic  30.6 us (6%)
  between operations  20 us (4%)
  blocking collectives  12.2 us (2%)
    dot_general x162, matrix products, convolve(): jnp.dot(columns, piece, preferred_element_type=jnp.float32)  71.3 us
    ppermute x20, waiting for transfers between devices, padded_2(): lax.ppermute(head, axis, [((i + 1) % count, i) for i in range(ends)])  70.4 us
    reshape x105, local copies, waits for them, and re-layouts, convolve(): piece = padded[:, offset_x:offset_x + size_x, offset_y:offset_y + size_y,...  69.7 us
    ppermute x20, starting transfers between devices, padded_2(): lax.ppermute(head, axis, [((i + 1) % count, i) for i in range(ends)])  63.2 us
    ppermute x20, starting transfers between devices, padded_2(): lax.ppermute(tail, axis, [(i, (i + 1) % count) for i in range(ends)])  59.5 us
    concatenate x25, other arithmetic, padded_2(): jnp.concatenate([lax.ppermute(tail, axis, [(i, (i + 1) % count) for i in...  25.9 us
    ppermute x20, waiting for transfers between devices, padded_2(): lax.ppermute(tail, axis, [(i, (i + 1) % count) for i in range(ends)])  21.8 us
    slice x43, local copies, waits for them, and re-layouts, convolve(): padded[:, offset_x:offset_x + size_x, offset_y:offset_y + size_y, offset_...  19 us
  transfers between devices with their start and end apart: 43, of which 34 were waited for; matrix products, arithmetic and copies ran while one was open for 7% of the time, Pallas kernels for 0%

commit v1 on v0

--- a/solution.py
+++ b/solution.py
@@ -115,7 +115,10 @@
         1, 3, 0, 2, 4, 5
     )
     outgoing_back = outgoing_back.reshape(planes, per_device, volume)
-    returned = lax.all_to_all(outgoing_back, ("gx", "gy"), split_axis=0, concat_axis=1, tiled=True)
+    devices = lax.axis_size(("gx", "gy"))
+    parts = jnp.stack(jnp.split(outgoing_back, devices, axis=0), axis=0)
+    parts = lax.all_to_all(parts, ("gx", "gy"), split_axis=0, concat_axis=0)
+    returned = jnp.concatenate(parts, axis=1)
     return returned.reshape(channels, size_x, size_y, size_z)
 
 

time: 496 us -> 537 us (1.083)
  local copies, waits for them, and re-layouts: 104 us -> 139 us
    unnamed x127 -> x241, local copies, waits for them, and re-layouts: 3.73 us -> 36.6 us
where the time goes in v1:
time: 537 us; the launch traced here: 527 us
  starting transfers between devices  141 us (26%)
  local copies, waits for them, and re-layouts  139 us (26%)
  waiting for transfers between devices  107 us (20%)
  matrix products  76.3 us (14%)
  other arithmetic  31.3 us (6%)
  between operations  20.5 us (4%)
  blocking collectives  12.1 us (2%)
    dot_general x162, matrix products, convolve(): jnp.dot(columns, piece, preferred_element_type=jnp.float32)  75.9 us
    reshape x105, local copies, waits for them, and re-layouts, convolve(): piece = padded[:, offset_x:offset_x + size_x, offset_y:offset_y + size_y,...  71.7 us
    ppermute x20, waiting for transfers between devices, padded_2(): lax.ppermute(head, axis, [((i + 1) % count, i) for i in range(ends)])  69.5 us
    ppermute x20, starting transfers between devices, padded_2(): lax.ppermute(head, axis, [((i + 1) % count, i) for i in range(ends)])  63.4 us
    ppermute x20, starting transfers between devices, padded_2(): lax.ppermute(tail, axis, [(i, (i + 1) % count) for i in range(ends)])  59.5 us
    unnamed x241, local copies, waits for them, and re-layouts  36.6 us
    concatenate x25, other arithmetic, padded_2(): jnp.concatenate([lax.ppermute(tail, axis, [(i, (i + 1) % count) for i in...  26.6 us
    ppermute x20, waiting for transfers between devices, padded_2(): lax.ppermute(tail, axis, [(i, (i + 1) % count) for i in range(ends)])  23.2 us
  transfers between devices with their start and end apart: 43, of which 34 were waited for; matrix products, arithmetic and copies ran while one was open for 7% of the time, Pallas kernels for 0%

profile of v1, /device:TPU:72, one launch (start us, length us, event | category | flops | bytes accessed | tf_op | source)
XLA Modules:
  0.0 526.9 jit_solution(5012515438667076121)
XLA Ops:
  2.9 4.5 collective-permute-start.1
  11.1 3.4 collective-permute-start.2
  19.6 4.5 collective-permute-done.3
  27.8 6.0 %collective-permute-start.4 = (bf16[32,6,6,1]{3,2,1,0:T(8,128)(2,1)}, bf16[32,6,6,1]{3,2,1,0:T(8,128)(2,1)}, u32[]{:S(2)}, u32[]{:S(2)}) collective-permute-start(bf16[32,6,6,1]{3,2,1,0:T(8,128)(2,1)} %get-tuple-element.112), channel_id=1, source_target_pairs={{0,1},{1,2},{2,3},{4,5},{5,6},{6,7},{8,9},{9,10},{10,11},{12,13},{... | collective-permute-start | bytes 6920 | tf_op jit(solution)/shard_map/ppermute | solution.py:15
  40.8 8.9 %collective-permute-done.5 = bf16[32,6,6,1]{3,2,1,0:T(8,128)(2,1)} collective-permute-done((bf16[32,6,6,1]{3,2,1,0:T(8,128)(2,1)}, bf16[32,6,6,1]{3,2,1,0:T(8,128)(2,1)}, u32[]{:S(2)}, u32[]{:S(2)}) %collective-permute-start.5) | collective-permute-done | bytes 2336 | tf_op jit(solution)/shard_map/ppermute | solution.py:17
  50.2 3.7 pad_maximum_fusion.2
  54.0 4.1 fusion.339
  102.0 4.5 collective-permute-start.7
  109.3 3.4 collective-permute-start.8
  117.3 4.1 collective-permute-done.9
  123.2 5.6 %collective-permute-start.10 = (bf16[32,6,6,1]{3,2,1,0:T(8,128)(2,1)}, bf16[32,6,6,1]{3,2,1,0:T(8,128)(2,1)}, u32[]{:S(2)}, u32[]{:S(2)}) collective-permute-start(bf16[32,6,6,1]{3,2,1,0:T(8,128)(2,1)} %get-tuple-element.107), channel_id=1, source_target_pairs={{0,1},{1,2},{2,3},{4,5},{5,6},{6,7},{8,9},{9,10},{10,11},{12,13},{... | collective-permute-start | bytes 6920 | tf_op jit(solution)/shard_map/ppermute | solution.py:15
  144.0 6.6 %collective-permute-done.11 = bf16[32,6,6,1]{3,2,1,0:T(8,128)(2,1)} collective-permute-done((bf16[32,6,6,1]{3,2,1,0:T(8,128)(2,1)}, bf16[32,6,6,1]{3,2,1,0:T(8,128)(2,1)}, u32[]{:S(2)}, u32[]{:S(2)}) %collective-permute-start.11) | collective-permute-done | bytes 2336 | tf_op jit(solution)/shard_map/ppermute | solution.py:17
  150.6 4.1 maximum_maximum_fusion.3
  178.3 3.4 fusion.338
  212.1 4.5 collective-permute-start.13
  218.7 3.1 collective-permute-start.14
  223.5 4.2 collective-permute-done.15
  227.8 3.2 collective-permute-start.16
  231.0 3.5 collective-permute-start.17
  235.6 5.0 collective-permute-done.17
  248.6 4.5 collective-permute-start.19
  255.2 2.5 collective-permute-start.20
  260.7 4.1 collective-permute-done.21
  268.2 5.1 collective-permute-start.23
  277.3 7.7 %collective-permute-done.23 = bf16[64,4,4,1]{3,2,1,0:T(4,128)(2,1)S(1)} collective-permute-done((bf16[64,4,4,1]{3,2,1,0:T(4,128)(2,1)S(1)}, bf16[64,4,4,1]{3,2,1,0:T(4,128)(2,1)S(1)}, u32[]{:S(2)}, u32[]{:S(2)}) %collective-permute-start.23) | collective-permute-done | bytes 2080 | tf_op jit(solution)/shard_map/ppermute | solution.py:17
  306.7 4.2 all-to-all-start
  331.1 4.8 collective-permute-start.25
  372.4 8.4 %all-to-all-start.1 = ((bf16[64,1,1,64]{3,2,1,0:T(2,128)(2,1)}), bf16[64,1,1,64]{3,2,1,0:T(2,128)(2,1)S(1)}, u32[]{:S(2)}, u32[]{:S(2)}) async-start(bf16[64,1,1,64]{3,2,1,0:T(2,128)(2,1)} %constant_dynamic-update-slice_fusion.9), calls=%async_computation.1 | async-start | bytes 65536 | tf_op jit(solution)/shard_map/all_to_all | solution.py:120
  380.8 7.0 %all-to-all-done.1 = bf16[64,1,1,64]{3,2,1,0:T(2,128)(2,1)S(1)} async-done(((bf16[64,1,1,64]{3,2,1,0:T(2,128)(2,1)}), bf16[64,1,1,64]{3,2,1,0:T(2,128)(2,1)S(1)}, u32[]{:S(2)}, u32[]{:S(2)}) %all-to-all-start.1) | async-done | bytes 8224 | tf_op jit(solution)/shard_map/all_to_all | solution.py:120
  388.7 5.6 %all-to-all-start.2 = ((bf16[1,128,64]{2,0,1:T(2,128)(2,1)}), bf16[1,128,64]{2,0,1:T(2,128)(2,1)S(1)}, u32[]{:S(2)}, u32[]{:S(2)}) async-start(bf16[1,128,64]{2,0,1:T(2,128)(2,1)} %copy.369), calls=%async_computation.2 | async-start | bytes 131072 | tf_op jit(solution)/shard_map/all_to_all | solution.py:103
  394.5 7.0 %all-to-all-done.2 = bf16[1,128,64]{2,0,1:T(2,128)(2,1)S(1)} async-done(((bf16[1,128,64]{2,0,1:T(2,128)(2,1)}), bf16[1,128,64]{2,0,1:T(2,128)(2,1)S(1)}, u32[]{:S(2)}, u32[]{:S(2)}) %all-to-all-start.2) | async-done | bytes 16416 | tf_op jit(solution)/shard_map/all_to_all | solution.py:103
  403.5 5.0 collective-permute-start.27
  408.6 3.2 collective-permute-done.27
  413.3 12.1 %all_to_all.28 = bf16[64,1,2,64]{3,2,1,0:T(2,128)(2,1)S(1)} all-to-all(bf16[64,1,2,64]{3,2,1,0:T(2,128)(2,1)S(1)} %constant_dynamic-update-slice_fusion.73), channel_id=1, replica_groups=mesh['gx'=16,'gy'=4,'gz'=4] {'gx','gy'}, dimensions={0} | all-to-all | bytes 32768 | tf_op jit(solution)/shard_map/all_to_all | solution.py:120
  427.6 4.5 collective-permute-start.29
  434.8 2.5 collective-permute-start.30
  438.9 4.2 collective-permute-done.30
  443.1 4.1 collective-permute-done.31
  447.3 3.7 collective-permute-start.33
  451.0 4.3 collective-permute-start.32
  468.0 4.5 collective-permute-start.35
  472.5 3.0 collective-permute-done.34
  476.7 2.5 collective-permute-start.36
  482.0 5.6 %collective-permute-done.36 = bf16[96,6,1,256]{0,3,2,1:T(8,128)(2,1)S(1)} collective-permute-done((bf16[96,6,1,256]{0,3,2,1:T(8,128)(2,1)S(1)}, bf16[96,6,1,256]{0,3,2,1:T(8,128)(2,1)S(1)}, u32[]{:S(2)}, u32[]{:S(2)}) %collective-permute-start.36) | collective-permute-done | bytes 294944 | tf_op jit(solution)/shard_map/ppermute | solution.py:15
  487.6 4.3 collective-permute-done.37
  492.0 5.5 %collective-permute-start.38 = (bf16[96,6,6,1]{0,3,2,1:T(2,128)(2,1)S(1)}, bf16[96,6,6,1]{0,3,2,1:T(2,128)(2,1)S(1)}, u32[]{:S(2)}, u32[]{:S(2)}) collective-permute-start(bf16[96,6,6,1]{0,3,2,1:T(2,128)(2,1)S(1)} %get-tuple-element.7), channel_id=1, source_target_pairs={{0,1},{1,2},{2,3},{4,5},{5,6},{6,7},{8,9},{9,10},{10,11},{12,13},{... | collective-permute-start | bytes 20744 | tf_op jit(solution)/shard_map/ppermute | solution.py:15
  505.3 4.2 maximum_maximum_fusion
  512.3 3.4 fusion.334
  (675 shorter events, 278.2 us)
Async XLA Ops:
  0.0 425.3 %copy-start = (bf16[128,128]{1,0:T(8,128)(2,1)S(1)}, bf16[128,128]{1,0:T(8,128)(2,1)}, u32[]{:S(2)}) copy-start(bf16[128,128]{1,0:T(8,128)(2,1)} %param.19) | copy-start | bytes 98308
  1.0 6.5 %collective-permute-start = (bf16[32,1,4,256]{3,2,1,0:T(4,128)(2,1)S(1)}, bf16[32,1,4,256]{3,2,1,0:T(4,128)(2,1)S(1)}, u32[]{:S(2)}, u32[]{:S(2)}) collective-permute-start(bf16[32,1,4,256]{3,2,1,0:T(4,128)(2,1)S(1)} %get-tuple-element.198), channel_id=1, source_target_pairs={{0,16},{16,32},{32,48},{48,64},{64,80},{80,96},{96,112},{112,128},... | collective-permute-start | bytes 196616 | tf_op jit(solution)/shard_map/ppermute | solution.py:15
  2.9 6.4 %collective-permute-start.1 = (bf16[32,1,4,256]{3,2,1,0:T(4,128)(2,1)S(1)}, bf16[32,1,4,256]{3,2,1,0:T(4,128)(2,1)S(1)}, u32[]{:S(2)}, u32[]{:S(2)}) collective-permute-start(bf16[32,1,4,256]{3,2,1,0:T(4,128)(2,1)S(1)} %get-tuple-element.197), channel_id=1, source_target_pairs={{16,0},{32,16},{48,32},{64,48},{80,64},{96,80},{112,96},{128,112},... | collective-permute-start | bytes 196616 | tf_op jit(solution)/shard_map/ppermute | solution.py:17
  11.1 8.5 %collective-permute-start.2 = (bf16[32,6,1,256]{3,2,1,0:T(2,128)(2,1)S(1)}, bf16[32,6,1,256]{3,2,1,0:T(2,128)(2,1)S(1)}, u32[]{:S(2)}, u32[]{:S(2)}) collective-permute-start(bf16[32,6,1,256]{3,2,1,0:T(2,128)(2,1)S(1)} %get-tuple-element.157), channel_id=1, source_target_pairs={{0,4},{4,8},{8,12},{1,5},{5,9},{9,13},{2,6},{6,10},{10,14},{3,7},{... | collective-permute-start | bytes 294920 | tf_op jit(solution)/shard_map/ppermute | solution.py:15
  14.5 9.6 %collective-permute-start.3 = (bf16[32,6,1,256]{3,2,1,0:T(2,128)(2,1)S(1)}, bf16[32,6,1,256]{3,2,1,0:T(2,128)(2,1)S(1)}, u32[]{:S(2)}, u32[]{:S(2)}) collective-permute-start(bf16[32,6,1,256]{3,2,1,0:T(2,128)(2,1)S(1)} %get-tuple-element.158), channel_id=1, source_target_pairs={{4,0},{8,4},{12,8},{5,1},{9,5},{13,9},{6,2},{10,6},{14,10},{7,3},{... | collective-permute-start | bytes 294920 | tf_op jit(solution)/shard_map/ppermute | solution.py:17
  25.9 23.8 %collective-permute-start.5 = (bf16[32,6,6,1]{3,2,1,0:T(8,128)(2,1)}, bf16[32,6,6,1]{3,2,1,0:T(8,128)(2,1)}, u32[]{:S(2)}, u32[]{:S(2)}) collective-permute-start(bf16[32,6,6,1]{3,2,1,0:T(8,128)(2,1)} %get-tuple-element.111), channel_id=1, source_target_pairs={{1,0},{2,1},{3,2},{5,4},{6,5},{7,6},{9,8},{10,9},{11,10},{13,12},{... | collective-permute-start | bytes 6920 | tf_op jit(solution)/shard_map/ppermute | solution.py:17
  27.8 22.5 %collective-permute-start.4 = (bf16[32,6,6,1]{3,2,1,0:T(8,128)(2,1)}, bf16[32,6,6,1]{3,2,1,0:T(8,128)(2,1)}, u32[]{:S(2)}, u32[]{:S(2)}) collective-permute-start(bf16[32,6,6,1]{3,2,1,0:T(8,128)(2,1)} %get-tuple-element.112), channel_id=1, source_target_pairs={{0,1},{1,2},{2,3},{4,5},{5,6},{6,7},{8,9},{9,10},{10,11},{12,13},{... | collective-permute-start | bytes 6920 | tf_op jit(solution)/shard_map/ppermute | solution.py:15
  100.0 6.7 %collective-permute-start.6 = (bf16[32,1,4,256]{3,2,1,0:T(4,128)(2,1)S(1)}, bf16[32,1,4,256]{3,2,1,0:T(4,128)(2,1)S(1)}, u32[]{:S(2)}, u32[]{:S(2)}) collective-permute-start(bf16[32,1,4,256]{3,2,1,0:T(4,128)(2,1)S(1)} %get-tuple-element.193), channel_id=1, source_target_pairs={{0,16},{16,32},{32,48},{48,64},{64,80},{80,96},{96,112},{112,128},... | collective-permute-start | bytes 196616 | tf_op jit(solution)/shard_map/ppermute | solution.py:15
  102.0 6.4 %collective-permute-start.7 = (bf16[32,1,4,256]{3,2,1,0:T(4,128)(2,1)S(1)}, bf16[32,1,4,256]{3,2,1,0:T(4,128)(2,1)S(1)}, u32[]{:S(2)}, u32[]{:S(2)}) collective-permute-start(bf16[32,1,4,256]{3,2,1,0:T(4,128)(2,1)S(1)} %get-tuple-element.192), channel_id=1, source_target_pairs={{16,0},{32,16},{48,32},{64,48},{80,64},{96,80},{112,96},{128,112},... | collective-permute-start | bytes 196616 | tf_op jit(solution)/shard_map/ppermute | solution.py:17
  109.3 8.1 %collective-permute-start.8 = (bf16[32,6,1,256]{3,2,1,0:T(2,128)(2,1)S(1)}, bf16[32,6,1,256]{3,2,1,0:T(2,128)(2,1)S(1)}, u32[]{:S(2)}, u32[]{:S(2)}) collective-permute-start(bf16[32,6,1,256]{3,2,1,0:T(2,128)(2,1)S(1)} %get-tuple-element.152), channel_id=1, source_target_pairs={{0,4},{4,8},{8,12},{1,5},{5,9},{9,13},{2,6},{6,10},{10,14},{3,7},{... | collective-permute-start | bytes 294920 | tf_op jit(solution)/shard_map/ppermute | solution.py:15
  112.7 8.8 %collective-permute-start.9 = (bf16[32,6,1,256]{3,2,1,0:T(2,128)(2,1)S(1)}, bf16[32,6,1,256]{3,2,1,0:T(2,128)(2,1)S(1)}, u32[]{:S(2)}, u32[]{:S(2)}) collective-permute-start(bf16[32,6,1,256]{3,2,1,0:T(2,128)(2,1)S(1)} %get-tuple-element.153), channel_id=1, source_target_pairs={{4,0},{8,4},{12,8},{5,1},{9,5},{13,9},{6,2},{10,6},{14,10},{7,3},{... | collective-permute-start | bytes 294920 | tf_op jit(solution)/shard_map/ppermute | solution.py:17
  117.3 26.6 %copy-start.11 = (bf16[32,6,1,256]{3,2,1,0:T(2,128)(2,1)}, bf16[32,6,1,256]{3,2,1,0:T(2,128)(2,1)S(1)}, u32[]{:S(2)}) copy-start(bf16[32,6,1,256]{3,2,1,0:T(2,128)(2,1)S(1)} %collective-permute-done.8) | copy-start | bytes 294916
  123.2 20.8 %collective-permute-start.10 = (bf16[32,6,6,1]{3,2,1,0:T(8,128)(2,1)}, bf16[32,6,6,1]{3,2,1,0:T(8,128)(2,1)}, u32[]{:S(2)}, u32[]{:S(2)}) collective-permute-start(bf16[32,6,6,1]{3,2,1,0:T(8,128)(2,1)} %get-tuple-element.107), channel_id=1, source_target_pairs={{0,1},{1,2},{2,3},{4,5},{5,6},{6,7},{8,9},{9,10},{10,11},{12,13},{... | collective-permute-start | bytes 6920 | tf_op jit(solution)/shard_map/ppermute | solution.py:15
  128.8 21.8 %collective-permute-start.11 = (bf16[32,6,6,1]{3,2,1,0:T(8,128)(2,1)}, bf16[32,6,6,1]{3,2,1,0:T(8,128)(2,1)}, u32[]{:S(2)}, u32[]{:S(2)}) collective-permute-start(bf16[32,6,6,1]{3,2,1,0:T(8,128)(2,1)} %get-tuple-element.108), channel_id=1, source_target_pairs={{1,0},{2,1},{3,2},{5,4},{6,5},{7,6},{9,8},{10,9},{11,10},{13,12},{... | collective-permute-start | bytes 6920 | tf_op jit(solution)/shard_map/ppermute | solution.py:17
  210.2 6.6 %collective-permute-start.12 = (bf16[32,1,2,128]{0,3,2,1:T(8,128)(2,1)S(1)}, bf16[32,1,2,128]{0,3,2,1:T(8,128)(2,1)S(1)}, u32[]{:S(2)}, u32[]{:S(2)}) collective-permute-start(bf16[32,1,2,128]{0,3,2,1:T(8,128)(2,1)S(1)} %get-tuple-element.208), channel_id=1, source_target_pairs={{0,16},{16,32},{32,48},{48,64},{64,80},{80,96},{96,112},{112,128},... | collective-permute-start | bytes 49160 | tf_op jit(solution)/shard_map/ppermute | solution.py:15
  212.1 6.4 %collective-permute-start.13 = (bf16[32,1,2,128]{0,3,2,1:T(8,128)(2,1)S(1)}, bf16[32,1,2,128]{0,3,2,1:T(8,128)(2,1)S(1)}, u32[]{:S(2)}, u32[]{:S(2)}) collective-permute-start(bf16[32,1,2,128]{0,3,2,1:T(8,128)(2,1)S(1)} %get-tuple-element.209), channel_id=1, source_target_pairs={{16,0},{32,16},{48,32},{64,48},{80,64},{96,80},{112,96},{128,112},... | collective-permute-start | bytes 49160 | tf_op jit(solution)/shard_map/ppermute | solution.py:17
  218.7 4.8 collective-permute-start.14
  221.8 5.8 %collective-permute-start.15 = (bf16[32,4,1,128]{3,0,2,1:T(8,128)(2,1)S(1)}, bf16[32,4,1,128]{3,0,2,1:T(8,128)(2,1)S(1)}, u32[]{:S(2)}, u32[]{:S(2)}) collective-permute-start(bf16[32,4,1,128]{3,0,2,1:T(8,128)(2,1)S(1)} %get-tuple-element.224), channel_id=1, source_target_pairs={{4,0},{8,4},{12,8},{5,1},{9,5},{13,9},{6,2},{10,6},{14,10},{7,3},{... | collective-permute-start | bytes 98312 | tf_op jit(solution)/shard_map/ppermute | solution.py:17
  227.8 7.9 %collective-permute-start.16 = (bf16[32,4,4,1]{3,0,2,1:T(8,128)(2,1)S(1)}, bf16[32,4,4,1]{3,0,2,1:T(8,128)(2,1)S(1)}, u32[]{:S(2)}, u32[]{:S(2)}) collective-permute-start(bf16[32,4,4,1]{3,0,2,1:T(8,128)(2,1)S(1)} %get-tuple-element.206), channel_id=1, source_target_pairs={{0,1},{1,2},{2,3},{4,5},{5,6},{6,7},{8,9},{9,10},{10,11},{12,13},{... | collective-permute-start | bytes 3080 | tf_op jit(solution)/shard_map/ppermute | solution.py:15
  231.0 9.6 %collective-permute-start.17 = (bf16[32,4,4,1]{3,0,2,1:T(8,128)(2,1)S(1)}, bf16[32,4,4,1]{3,0,2,1:T(8,128)(2,1)S(1)}, u32[]{:S(2)}, u32[]{:S(2)}) collective-permute-start(bf16[32,4,4,1]{3,0,2,1:T(8,128)(2,1)S(1)} %get-tuple-element.207), channel_id=1, source_target_pairs={{1,0},{2,1},{3,2},{5,4},{6,5},{7,6},{9,8},{10,9},{11,10},{13,12},{... | collective-permute-start | bytes 3080 | tf_op jit(solution)/shard_map/ppermute | solution.py:17
  246.7 6.5 %collective-permute-start.18 = (bf16[64,1,2,128]{3,2,1,0:T(2,128)(2,1)S(1)}, bf16[64,1,2,128]{3,2,1,0:T(2,128)(2,1)S(1)}, u32[]{:S(2)}, u32[]{:S(2)}) collective-permute-start(bf16[64,1,2,128]{3,2,1,0:T(2,128)(2,1)S(1)} %get-tuple-element.220), channel_id=1, source_target_pairs={{0,16},{16,32},{32,48},{48,64},{64,80},{80,96},{96,112},{112,128},... | collective-permute-start | bytes 98312 | tf_op jit(solution)/shard_map/ppermute | solution.py:15
  248.6 6.1 %collective-permute-start.19 = (bf16[64,1,2,128]{3,2,1,0:T(2,128)(2,1)S(1)}, bf16[64,1,2,128]{3,2,1,0:T(2,128)(2,1)S(1)}, u32[]{:S(2)}, u32[]{:S(2)}) collective-permute-start(bf16[64,1,2,128]{3,2,1,0:T(2,128)(2,1)S(1)} %get-tuple-element.219), channel_id=1, source_target_pairs={{16,0},{32,16},{48,32},{64,48},{80,64},{96,80},{112,96},{128,112},... | collective-permute-start | bytes 98312 | tf_op jit(solution)/shard_map/ppermute | solution.py:17
  255.2 5.5 %collective-permute-start.20 = (bf16[64,4,1,128]{3,2,1,0:T(2,128)(2,1)S(1)}, bf16[64,4,1,128]{3,2,1,0:T(2,128)(2,1)S(1)}, u32[]{:S(2)}, u32[]{:S(2)}) collective-permute-start(bf16[64,4,1,128]{3,2,1,0:T(2,128)(2,1)S(1)} %get-tuple-element.202), channel_id=1, source_target_pairs={{0,4},{4,8},{8,12},{1,5},{5,9},{9,13},{2,6},{6,10},{10,14},{3,7},{... | collective-permute-start | bytes 196616 | tf_op jit(solution)/shard_map/ppermute | solution.py:15
  257.7 7.1 %collective-permute-start.21 = (bf16[64,4,1,128]{3,2,1,0:T(2,128)(2,1)S(1)}, bf16[64,4,1,128]{3,2,1,0:T(2,128)(2,1)S(1)}, u32[]{:S(2)}, u32[]{:S(2)}) collective-permute-start(bf16[64,4,1,128]{3,2,1,0:T(2,128)(2,1)S(1)} %get-tuple-element.203), channel_id=1, source_target_pairs={{4,0},{8,4},{12,8},{5,1},{9,5},{13,9},{6,2},{10,6},{14,10},{7,3},{... | collective-permute-start | bytes 196616 | tf_op jit(solution)/shard_map/ppermute | solution.py:17
  266.2 11.1 %collective-permute-start.22 = (bf16[64,4,4,1]{3,2,1,0:T(4,128)(2,1)}, bf16[64,4,4,1]{3,2,1,0:T(4,128)(2,1)S(1)}, u32[]{:S(2)}, u32[]{:S(2)}) collective-permute-start(bf16[64,4,4,1]{3,2,1,0:T(4,128)(2,1)} %get-tuple-element.169), channel_id=1, source_target_pairs={{0,1},{1,2},{2,3},{4,5},{5,6},{6,7},{8,9},{9,10},{10,11},{12,13},{... | collective-permute-start | bytes 6152 | tf_op jit(solution)/shard_map/ppermute | solution.py:15
  268.2 16.8 %collective-permute-start.23 = (bf16[64,4,4,1]{3,2,1,0:T(4,128)(2,1)S(1)}, bf16[64,4,4,1]{3,2,1,0:T(4,128)(2,1)S(1)}, u32[]{:S(2)}, u32[]{:S(2)}) collective-permute-start(bf16[64,4,4,1]{3,2,1,0:T(4,128)(2,1)S(1)} %get-tuple-element.170), channel_id=1, source_target_pairs={{1,0},{2,1},{3,2},{5,4},{6,5},{7,6},{9,8},{10,9},{11,10},{13,12},{... | collective-permute-start | bytes 6152 | tf_op jit(solution)/shard_map/ppermute | solution.py:17
  303.8 84.0 %copy-start.54 = (bf16[128,64]{0,1:T(8,128)(2,1)S(1)}, bf16[128,64]{0,1:T(8,128)(2,1)}, u32[]{:S(2)}) copy-start(bf16[128,64]{0,1:T(8,128)(2,1)} %param.17) | copy-start | bytes 49156
  304.0 90.3 %copy-start.53 = (bf16[128,27]{0,1:T(8,128)(2,1)S(1)}, bf16[128,27]{0,1:T(8,128)(2,1)}, u32[]{:S(2)}) copy-start(bf16[128,27]{0,1:T(8,128)(2,1)} %param.18) | copy-start | bytes 20740
  306.0 126.1 %copy-start.15 = (bf16[64,5184]{1,0:T(8,128)(2,1)S(1)}, bf16[64,5184]{1,0:T(8,128)(2,1)}, u32[]{:S(2)}) copy-start(bf16[64,5184]{1,0:T(8,128)(2,1)} %param.20) | copy-start | bytes 1990660
  306.7 22.4 %all-to-all-start = ((bf16[1,64,64]{2,0,1:T(2,128)(2,1)}), bf16[1,64,64]{2,0,1:T(2,128)(2,1)S(1)}, u32[]{:S(2)}, u32[]{:S(2)}) async-start(bf16[1,64,64]{2,0,1:T(2,128)(2,1)} %copy.368), calls=%async_computation | async-start | bytes 65536 | tf_op jit(solution)/shard_map/all_to_all | solution.py:103
  329.2 7.4 %collective-permute-start.24 = (bf16[1,16,4,1]{3,2,1,0:T(4,128)(2,1)S(1)}, bf16[1,16,4,1]{3,2,1,0:T(4,128)(2,1)S(1)}, u32[]{:S(2)}, u32[]{:S(2)}) collective-permute-start(bf16[1,16,4,1]{3,2,1,0:T(4,128)(2,1)S(1)} %get-tuple-element.293), channel_id=1, source_target_pairs={{0,1},{1,2},{2,3},{4,5},{5,6},{6,7},{8,9},{9,10},{10,11},{12,13},{... | collective-permute-start | bytes 392 | tf_op jit(solution)/shard_map/ppermute | solution.py:15
  331.1 7.8 %collective-permute-start.25 = (bf16[1,16,4,1]{3,2,1,0:T(4,128)(2,1)S(1)}, bf16[1,16,4,1]{3,2,1,0:T(4,128)(2,1)S(1)}, u32[]{:S(2)}, u32[]{:S(2)}) collective-permute-start(bf16[1,16,4,1]{3,2,1,0:T(4,128)(2,1)S(1)} %get-tuple-element.294), channel_id=1, source_target_pairs={{1,0},{2,1},{3,2},{5,4},{6,5},{7,6},{9,8},{10,9},{11,10},{13,12},{... | collective-permute-start | bytes 392 | tf_op jit(solution)/shard_map/ppermute | solution.py:17
  372.4 15.4 %all-to-all-start.1 = ((bf16[64,1,1,64]{3,2,1,0:T(2,128)(2,1)}), bf16[64,1,1,64]{3,2,1,0:T(2,128)(2,1)S(1)}, u32[]{:S(2)}, u32[]{:S(2)}) async-start(bf16[64,1,1,64]{3,2,1,0:T(2,128)(2,1)} %constant_dynamic-update-slice_fusion.9), calls=%async_computation.1 | async-start | bytes 65536 | tf_op jit(solution)/shard_map/all_to_all | solution.py:120
  388.7 12.7 %all-to-all-start.2 = ((bf16[1,128,64]{2,0,1:T(2,128)(2,1)}), bf16[1,128,64]{2,0,1:T(2,128)(2,1)S(1)}, u32[]{:S(2)}, u32[]{:S(2)}) async-start(bf16[1,128,64]{2,0,1:T(2,128)(2,1)} %copy.369), calls=%async_computation.2 | async-start | bytes 131072 | tf_op jit(solution)/shard_map/all_to_all | solution.py:103
  401.6 7.0 %collective-permute-start.26 = (bf16[2,16,4,1]{3,1,2,0:T(8,128)(2,1)S(1)}, bf16[2,16,4,1]{3,1,2,0:T(8,128)(2,1)S(1)}, u32[]{:S(2)}, u32[]{:S(2)}) collective-permute-start(bf16[2,16,4,1]{3,1,2,0:T(8,128)(2,1)S(1)} %get-tuple-element.289), channel_id=1, source_target_pairs={{0,1},{1,2},{2,3},{4,5},{5,6},{6,7},{8,9},{9,10},{10,11},{12,13},{... | collective-permute-start | bytes 776 | tf_op jit(solution)/shard_map/ppermute | solution.py:15
  403.5 8.3 %collective-permute-start.27 = (bf16[2,16,4,1]{3,1,2,0:T(8,128)(2,1)S(1)}, bf16[2,16,4,1]{3,1,2,0:T(8,128)(2,1)S(1)}, u32[]{:S(2)}, u32[]{:S(2)}) collective-permute-start(bf16[2,16,4,1]{3,1,2,0:T(8,128)(2,1)S(1)} %get-tuple-element.290), channel_id=1, source_target_pairs={{1,0},{2,1},{3,2},{5,4},{6,5},{7,6},{9,8},{10,9},{11,10},{13,12},{... | collective-permute-start | bytes 776 | tf_op jit(solution)/shard_map/ppermute | solution.py:17
  425.6 7.2 %collective-permute-start.28 = (bf16[192,1,2,128]{0,3,2,1:T(8,128)(2,1)S(1)}, bf16[192,1,2,128]{0,3,2,1:T(8,128)(2,1)S(1)}, u32[]{:S(2)}, u32[]{:S(2)}) collective-permute-start(bf16[192,1,2,128]{0,3,2,1:T(8,128)(2,1)S(1)} %get-tuple-element.161), channel_id=1, source_target_pairs={{0,16},{16,32},{32,48},{48,64},{64,80},{80,96},{96,112},{112,128},... | collective-permute-start | bytes 294920 | tf_op jit(solution)/shard_map/ppermute | solution.py:15
  427.6 7.0 %collective-permute-start.29 = (bf16[192,1,2,128]{0,3,2,1:T(8,128)(2,1)S(1)}, bf16[192,1,2,128]{0,3,2,1:T(8,128)(2,1)S(1)}, u32[]{:S(2)}, u32[]{:S(2)}) collective-permute-start(bf16[192,1,2,128]{0,3,2,1:T(8,128)(2,1)S(1)} %get-tuple-element.162), channel_id=1, source_target_pairs={{16,0},{32,16},{48,32},{64,48},{80,64},{96,80},{112,96},{128,112},... | collective-permute-start | bytes 294920 | tf_op jit(solution)/shard_map/ppermute | solution.py:17
  434.8 8.3 %collective-permute-start.30 = (bf16[192,4,1,128]{0,3,2,1:T(8,128)(2,1)S(1)}, bf16[192,4,1,128]{0,3,2,1:T(8,128)(2,1)S(1)}, u32[]{:S(2)}, u32[]{:S(2)}) collective-permute-start(bf16[192,4,1,128]{0,3,2,1:T(8,128)(2,1)S(1)} %get-tuple-element.127), channel_id=1, source_target_pairs={{0,4},{4,8},{8,12},{1,5},{5,9},{9,13},{2,6},{6,10},{10,14},{3,7},{... | collective-permute-start | bytes 589832 | tf_op jit(solution)/shard_map/ppermute | solution.py:15
  437.3 10.0 %collective-permute-start.31 = (bf16[192,4,1,128]{0,3,2,1:T(8,128)(2,1)S(1)}, bf16[192,4,1,128]{0,3,2,1:T(8,128)(2,1)S(1)}, u32[]{:S(2)}, u32[]{:S(2)}) collective-permute-start(bf16[192,4,1,128]{0,3,2,1:T(8,128)(2,1)S(1)} %get-tuple-element.128), channel_id=1, source_target_pairs={{4,0},{8,4},{12,8},{5,1},{9,5},{13,9},{6,2},{10,6},{14,10},{7,3},{... | collective-permute-start | bytes 589832 | tf_op jit(solution)/shard_map/ppermute | solution.py:17
  447.3 8.6 %collective-permute-start.33 = (bf16[192,4,4,1]{0,2,3,1:T(4,128)(2,1)S(1)}, bf16[192,4,4,1]{0,2,3,1:T(4,128)(2,1)S(1)}, u32[]{:S(2)}, u32[]{:S(2)}) collective-permute-start(bf16[192,4,4,1]{0,2,3,1:T(4,128)(2,1)S(1)} %copy.377), channel_id=1, source_target_pairs={{1,0},{2,1},{3,2},{5,4},{6,5},{7,6},{9,8},{10,9},{11,10},{13,12},{... | collective-permute-start | bytes 18440 | tf_op jit(solution)/shard_map/ppermute | solution.py:17
  451.0 6.4 %collective-permute-start.32 = (bf16[192,4,4,1]{0,2,3,1:T(4,128)(2,1)S(1)}, bf16[192,4,4,1]{0,2,3,1:T(4,128)(2,1)S(1)}, u32[]{:S(2)}, u32[]{:S(2)}) collective-permute-start(bf16[192,4,4,1]{0,2,3,1:T(4,128)(2,1)S(1)} %copy.373), channel_id=1, source_target_pairs={{0,1},{1,2},{2,3},{4,5},{5,6},{6,7},{8,9},{9,10},{10,11},{12,13},{... | collective-permute-start | bytes 18440 | tf_op jit(solution)/shard_map/ppermute | solution.py:15
  466.0 9.5 %collective-permute-start.34 = (bf16[96,1,4,256]{0,3,2,1:T(8,128)(2,1)S(1)}, bf16[96,1,4,256]{0,3,2,1:T(8,128)(2,1)S(1)}, u32[]{:S(2)}, u32[]{:S(2)}) collective-permute-start(bf16[96,1,4,256]{0,3,2,1:T(8,128)(2,1)S(1)} %get-tuple-element.33), channel_id=1, source_target_pairs={{0,16},{16,32},{32,48},{48,64},{64,80},{80,96},{96,112},{112,128},... | collective-permute-start | bytes 589832 | tf_op jit(solution)/shard_map/ppermute | solution.py:15
  468.0 8.4 %collective-permute-start.35 = (bf16[96,1,4,256]{0,3,2,1:T(8,128)(2,1)S(1)}, bf16[96,1,4,256]{0,3,2,1:T(8,128)(2,1)S(1)}, u32[]{:S(2)}, u32[]{:S(2)}) collective-permute-start(bf16[96,1,4,256]{0,3,2,1:T(8,128)(2,1)S(1)} %get-tuple-element.34), channel_id=1, source_target_pairs={{16,0},{32,16},{48,32},{64,48},{80,64},{96,80},{112,96},{128,112},... | collective-permute-start | bytes 589832 | tf_op jit(solution)/shard_map/ppermute | solution.py:17
  476.7 10.9 %collective-permute-start.36 = (bf16[96,6,1,256]{0,3,2,1:T(8,128)(2,1)S(1)}, bf16[96,6,1,256]{0,3,2,1:T(8,128)(2,1)S(1)}, u32[]{:S(2)}, u32[]{:S(2)}) collective-permute-start(bf16[96,6,1,256]{0,3,2,1:T(8,128)(2,1)S(1)} %get-tuple-element.11), channel_id=1, source_target_pairs={{0,4},{4,8},{8,12},{1,5},{5,9},{9,13},{2,6},{6,10},{10,14},{3,7},{... | collective-permute-start | bytes 884744 | tf_op jit(solution)/shard_map/ppermute | solution.py:15
  479.3 12.6 %collective-permute-start.37 = (bf16[96,6,1,256]{0,3,2,1:T(8,128)(2,1)S(1)}, bf16[96,6,1,256]{0,3,2,1:T(8,128)(2,1)S(1)}, u32[]{:S(2)}, u32[]{:S(2)}) collective-permute-start(bf16[96,6,1,256]{0,3,2,1:T(8,128)(2,1)S(1)} %get-tuple-element.12), channel_id=1, source_target_pairs={{4,0},{8,4},{12,8},{5,1},{9,5},{13,9},{6,2},{10,6},{14,10},{7,3},{... | collective-permute-start | bytes 884744 | tf_op jit(solution)/shard_map/ppermute | solution.py:17
  492.0 12.1 %collective-permute-start.38 = (bf16[96,6,6,1]{0,3,2,1:T(2,128)(2,1)S(1)}, bf16[96,6,6,1]{0,3,2,1:T(2,128)(2,1)S(1)}, u32[]{:S(2)}, u32[]{:S(2)}) collective-permute-start(bf16[96,6,6,1]{0,3,2,1:T(2,128)(2,1)S(1)} %get-tuple-element.7), channel_id=1, source_target_pairs={{0,1},{1,2},{2,3},{4,5},{5,6},{6,7},{8,9},{9,10},{10,11},{12,13},{... | collective-permute-start | bytes 20744 | tf_op jit(solution)/shard_map/ppermute | solution.py:15
  497.5 7.8 %collective-permute-start.39 = (bf16[96,6,6,1]{0,3,2,1:T(2,128)(2,1)S(1)}, bf16[96,6,6,1]{0,3,2,1:T(2,128)(2,1)S(1)}, u32[]{:S(2)}, u32[]{:S(2)}) collective-permute-start(bf16[96,6,6,1]{0,3,2,1:T(2,128)(2,1)S(1)} %get-tuple-element.8), channel_id=1, source_target_pairs={{1,0},{2,1},{3,2},{5,4},{6,5},{7,6},{9,8},{10,9},{11,10},{13,12},{... | collective-permute-start | bytes 20744 | tf_op jit(solution)/shard_map/ppermute | solution.py:17
  (50 other events, 209.4 us)
